TPU v7x, 32 devices: a whole 2x2x4 slice. The times are simulated.
32 devices in a mesh: groups: 2 (over x), rows: 8 (over z, y), chan: 2 (over core).
Axes of the slice: x: 2, y: 2, z: 4, core: 2. Of those that a mesh axis runs over, the one named last changes fastest.
Arguments:
- latents: bfloat16 [48, 32, 1024], P('groups', 'rows', 'chan'), parts along dimension 0, may hold values from -6 to 6
- timestep: int32 [6], P('groups'), parts along dimension 0, may hold values from 0 to 999
- label: int32 [6], P('groups'), parts along dimension 0, may hold values from 0 to 15
- time_table: bfloat16 [1000, 1024], P(None, 'chan'), may hold values from -3 to 3
- class_table: bfloat16 [16, 1024], replicated, may hold values from -6 to 6
- dw_kernel: bfloat16 [7, 7, 1024], P(None, None, 'chan'), may hold values from -0.875 to 0.875
- dw_bias: bfloat16 [1024], P('chan'), may hold values from -3 to 3
- ln_gain: bfloat16 [1024], P('chan'), may hold values from 0.25 to 1.75
- ln_bias: bfloat16 [1024], P('chan'), may hold values from -2 to 2
- up_weight: bfloat16 [1024, 4096], P(None, 'chan'), may hold values from -0.1875 to 0.1875
- up_bias: bfloat16 [4096], P('chan'), may hold values from -3 to 3
- down_weight: bfloat16 [4096, 1024], P('chan'), may hold values from -0.09375 to 0.09375
- down_bias: bfloat16 [1024], P('chan'), may hold values from -3 to 3
- layer_scale: bfloat16 [1024], replicated, may hold values from 0.5 to 1.5
Outputs:
- features: bfloat16 [48, 32, 1024], P(('groups', 'rows'), None, 'chan'), parts along dimension 0
- gradient: float32 [48, 32, 1024], P('groups', 'rows', 'chan'), parts along dimension 0
There are 2 independent parts, one for each index of `groups`. A program takes and returns all parts, laid end to end along the dimension named above; an argument that names none is the same for every part. Nothing has to cross between parts.
Inputs may be any that keep to these rules, and one draw needn't show every extreme that they name: One timestep index for each image, a row of the table of 1000 timesteps. `label`: one defect class for each image, out of 16 classes.
All inputs are finite; a program needn't handle non-finite values.
Results may differ from a plain program's by a relative error of at most 0.0045.
Values may be sent and summed in bfloat16 or wider, within the bound.
No kernel may reach another device: no remote copies, remote signals or barrier semaphores. Data moves between devices by JAX's collectives and lax.ppermute only.
A program may use at most 128 MiB of HBM per device.

v0:
```python
import jax
import jax.numpy as jnp
from jax import lax
from jax.sharding import PartitionSpec as P

KAPPA = 0.7978845608028654
EPSILON = 1e-06


def with_halo(cells, sides, width):
    for axis, dim in sides:
        count = lax.axis_size(axis)
        ends = count - 1
        head = lax.slice_in_dim(cells, 0, width, axis=dim)
        tail = lax.slice_in_dim(cells, cells.shape[dim] - width, cells.shape[dim], axis=dim)
        cells = jnp.concatenate(
            [
                lax.ppermute(tail, axis, [(i, (i + 1) % count) for i in range(ends)]),
                cells,
                lax.ppermute(head, axis, [((i + 1) % count, i) for i in range(ends)]),
            ],
            axis=dim,
        )
    return cells


def gelu_tanh(values):
    inner = KAPPA * (values + 0.044715 * values * values * values)
    return 0.5 * values * (1.0 + jnp.tanh(inner))


def gelu_slope(values):
    tangent = jnp.tanh(KAPPA * (values + 0.044715 * values * values * values))
    return 0.5 * (1.0 + tangent) + 0.5 * values * (1.0 - tangent * tangent) * KAPPA * (
        1.0 + 3.0 * 0.044715 * values * values
    )


def stencil(padded, kernel, masks):
    height = padded.shape[0] - 6
    width = padded.shape[1] - 6
    total = jnp.zeros((height, width, padded.shape[2]), jnp.float32)
    for row_tap in range(7):
        partial_row = jnp.zeros((height, width, padded.shape[2]), jnp.float32)
        for col_tap in range(7):
            partial_row = (
                partial_row
                + padded[row_tap : row_tap + height, col_tap : col_tap + width, :]
                * kernel[row_tap, col_tap]
            )
        total = total + partial_row * masks[row_tap][:, None, None]
    return total


def exact_dot(left, right):
    return jnp.dot(left, right, precision=lax.Precision.HIGHEST, preferred_element_type=jnp.float32)


def local_block(
    latent_pad,
    row_first,
    col_first,
    total_rows,
    total_cols,
    pad_grad,
    time_rows,
    class_half,
    slope_image,
    scale_half,
    dw_kernel,
    dw_bias,
    ln_gain,
    ln_bias,
    up_weight,
    up_bias,
    down_weight,
    down_bias,
    full_channels,
):
    pad_rows = latent_pad.shape[0]
    pad_cols = latent_pad.shape[1]
    height = pad_rows - 6
    width = pad_cols - 6
    channels = latent_pad.shape[2]
    images = time_rows.shape[0]
    image_height = total_rows // images
    row_global = row_first - 3 + jnp.arange(pad_rows, dtype=jnp.int32)
    row_image = jnp.floor_divide(row_global, image_height)
    col_global = col_first - 3 + jnp.arange(pad_cols, dtype=jnp.int32)
    col_valid = ((col_global >= 0) & (col_global < total_cols)).astype(jnp.float32)
    image_hot = (row_image[:, None] == jnp.arange(images, dtype=jnp.int32)[None, :]).astype(
        jnp.float32
    )
    time_pad = exact_dot(image_hot, time_rows)
    start_pad = latent_pad.astype(jnp.float32) + time_pad[:, None, :] * col_valid[None, :, None]
    masks = jnp.stack(
        [
            (row_image[tap : tap + height] == row_image[3 : 3 + height]).astype(jnp.float32)
            for tap in range(7)
        ]
    )
    kernel = dw_kernel.astype(jnp.float32)
    mixed = stencil(start_pad, kernel, masks) + dw_bias.astype(jnp.float32)
    tokens = height * width
    flat = mixed.reshape(tokens, channels)
    first_sum, second_sum = lax.psum((jnp.sum(flat, 1), jnp.sum(flat * flat, 1)), "chan")
    mean = first_sum / full_channels
    variance = second_sum / full_channels - mean * mean
    inverse = lax.rsqrt(variance + EPSILON)
    normed = (flat - mean[:, None]) * inverse[:, None]
    gain = ln_gain.astype(jnp.float32)
    scaled = (normed * gain + ln_bias.astype(jnp.float32)).astype(jnp.bfloat16)
    hidden = jnp.dot(
        lax.all_gather(scaled, "chan", axis=1, tiled=True),
        up_weight,
        preferred_element_type=jnp.float32,
    )
    hidden = hidden + up_bias.astype(jnp.float32)
    active = gelu_tanh(hidden).astype(jnp.bfloat16)
    branch = lax.psum_scatter(
        jnp.dot(active, down_weight, preferred_element_type=jnp.float32),
        "chan",
        scatter_dimension=1,
        tiled=True,
    )
    branch = branch + down_bias.astype(jnp.float32)
    start_cells = start_pad[3 : 3 + height, 3 : 3 + width].reshape(tokens, channels)
    features = (
        (start_cells + scale_half * branch).astype(jnp.bfloat16).reshape(height, width, channels)
    )
    token_image = image_hot[3 : 3 + height]
    slope_rows = exact_dot(token_image, slope_image)
    slope_tokens = jnp.broadcast_to(
        slope_rows[:, None, :], (height, width, slope_rows.shape[1])
    ).reshape(tokens, slope_rows.shape[1])
    hidden_grad = (slope_tokens * gelu_slope(hidden)).astype(jnp.bfloat16)
    grad_terms = lax.dot_general(
        hidden_grad, up_weight, (((1,), (1,)), ((), ())), preferred_element_type=jnp.float32
    )
    normed_grad = lax.psum_scatter(
        grad_terms.astype(jnp.bfloat16), "chan", scatter_dimension=1, tiled=True
    ).astype(jnp.float32)
    gained = normed_grad * gain
    grad_first, grad_second = lax.psum((jnp.sum(gained, 1), jnp.sum(gained * normed, 1)), "chan")
    mixed_grad = inverse[:, None] * (
        gained - grad_first[:, None] / full_channels - normed * grad_second[:, None] / full_channels
    )
    grad_pad = pad_grad(mixed_grad.reshape(height, width, channels))
    class_tokens = exact_dot(token_image, class_half)
    gradient = stencil(grad_pad, kernel[::-1, ::-1], masks) + class_tokens[:, None, :]
    return (features, gradient)


def per_device(
    latents,
    timestep,
    label,
    time_table,
    class_table,
    dw_kernel,
    dw_bias,
    ln_gain,
    ln_bias,
    up_weight,
    up_bias,
    down_weight,
    down_bias,
    layer_scale,
):
    channels = ln_gain.shape[0]
    full_channels = class_table.shape[1]
    half_index = lax.axis_index("chan")
    scale_full = layer_scale.astype(jnp.float32)
    scale_half = lax.dynamic_slice_in_dim(scale_full, half_index * channels, channels, 0)
    time_hot = (
        timestep[:, None] == jnp.arange(time_table.shape[0], dtype=jnp.int32)[None, :]
    ).astype(jnp.float32)
    time_rows = exact_dot(time_hot, time_table.astype(jnp.float32))
    class_hot = (
        label[:, None] == jnp.arange(class_table.shape[0], dtype=jnp.int32)[None, :]
    ).astype(jnp.float32)
    class_rows = exact_dot(class_hot, class_table.astype(jnp.float32))
    class_half = lax.dynamic_slice_in_dim(class_rows, half_index * channels, channels, 1)
    direction = (class_rows * scale_full).astype(jnp.bfloat16)
    slope_image = lax.dot_general(
        direction, down_weight, (((1,), (1,)), ((), ())), preferred_element_type=jnp.float32
    )
    latent_rows = lax.all_to_all(latents, "rows", split_axis=0, concat_axis=1, tiled=True)
    height = latent_rows.shape[0]
    width = latent_rows.shape[1]
    row_first = lax.axis_index("rows") * height
    col_first = 0
    total_rows = height * lax.axis_size("rows")
    latent_pad = with_halo(latent_rows, (("rows", 0),), 3)
    latent_pad = jnp.pad(latent_pad, ((0, 0), (3, 3), (0, 0)))

    def pad_grad(field):
        padded = with_halo(field.astype(jnp.bfloat16), (("rows", 0),), 3).astype(field.dtype)
        return jnp.pad(padded, ((0, 0), (3, 3), (0, 0)))

    features, gradient = local_block(
        latent_pad,
        row_first,
        col_first,
        total_rows,
        width,
        pad_grad,
        time_rows,
        class_half,
        slope_image,
        scale_half,
        dw_kernel,
        dw_bias,
        ln_gain,
        ln_bias,
        up_weight,
        up_bias,
        down_weight,
        down_bias,
        full_channels,
    )
    gradient = lax.all_to_all(gradient, "rows", split_axis=1, concat_axis=0, tiled=True)
    return (features, gradient)


def solution(mesh):
    in_specs = (
        P("groups", "rows", "chan"),
        P("groups"),
        P("groups"),
        P(None, "chan"),
        P(),
        P(None, None, "chan"),
        P("chan"),
        P("chan"),
        P("chan"),
        P(None, "chan"),
        P("chan"),
        P("chan", None),
        P("chan"),
        P(),
    )
    out_specs = (P(("groups", "rows"), None, "chan"), P("groups", "rows", "chan"))
    return jax.shard_map(
        per_device, mesh=mesh, in_specs=in_specs, out_specs=out_specs, check_vma=False
    )
```

profile of v0, /device:TPU:0, one launch (start us, length us, event | category | flops | bytes accessed | tf_op | source)
XLA Modules:
  0.0 107.5 jit_solution(14234665979605698154)
XLA Ops:
  7.2 7.5 %all-to-all-start = ((bf16[24,4,512]{2,1,0:T(4,128)(2,1)}), bf16[24,4,512]{2,1,0:T(4,128)(2,1)S(1)}, u32[]{:S(2)}, u32[]{:S(2)}) async-start(bf16[24,4,512]{2,1,0:T(4,128)(2,1)} %param.14), calls=%async_computation | async-start | bytes 196608 | tf_op jit(solution)/shard_map/all_to_all | solution.py:188
  14.7 1.0 fusion.184
  15.8 1.1 %fusion.183 = (f32[1,1,512]{2,1,0:T(1,128)S(1)}, f32[1,1,512]{2,1,0:T(1,128)S(1)}, f32[1,1,512]{2,1,0:T(1,128)S(1)}, f32[1,1,512]{2,1,0:T(1,128)S(1)}, f32[1,1,5...) fusion(bf16[7,7,512]{2,1,0:T(8,128)(2,1)} %param.19), kind=kLoop, calls=%fused_computation.314 | loop fusion | bytes 77824 | tf_op jit(solution)/shard_map/slice | solution.py:49
  17.1 1.6 %fusion.182 = (f32[1,1,512]{2,1,0:T(1,128)S(1)}, f32[1,1,512]{2,1,0:T(1,128)S(1)}, f32[1,1,512]{2,1,0:T(1,128)S(1)}, f32[1,1,512]{2,1,0:T(1,128)S(1)}, f32[1,1,5...) fusion(bf16[7,7,512]{2,1,0:T(8,128)(2,1)} %param.19), kind=kLoop, calls=%fused_computation.313 | loop fusion | bytes 77824 | tf_op jit(solution)/shard_map/slice | solution.py:49
  18.9 0.7 convert_element_type.102
  19.6 0.7 convert_element_type.101
  20.3 0.7 convert_element_type.103
  21.0 0.7 convert_element_type.93
  21.7 0.7 convert_element_type.105
  22.4 0.9 fusion.163
  23.3 0.2 fusion.179
  23.5 0.2 fusion.169
  23.7 3.4 %fusion.164 = f32[3,2048]{1,0:T(4,128)S(1)} fusion(bf16[2048,1024]{1,0:T(8,128)(2,1)} %param.25, f32[3,1024]{1,0:T(4,128)S(1)} %fusion.169, f32[1024]{0:T(1024)S(1)} %convert_element_type.93), kind=kOutput, calls=%fused_computation.280 | convolution fusion | flops 12589056 | bytes 4235264 | tf_op jit(solution)/shard_map/dot_general | solution.py:185
  27.1 0.2 fusion.171
  27.3 0.7 compare_convert_fusion.5
  28.0 1.3 %collective-permute-start.1 = (bf16[3,32,512]{2,0,1:T(4,128)(2,1)S(1)}, bf16[3,32,512]{2,0,1:T(4,128)(2,1)S(1)}, u32[]{:S(2)}, u32[]{:S(2)}) collective-permute-start(bf16[3,32,512]{2,0,1:T(4,128)(2,1)S(1)} %bitcast.86), channel_id=1, source_target_pairs={{2,0},{4,2},{6,4},{8,6},{10,8},{12,10},{14,12},{3,1},{5,3},{7,5},{... | collective-permute-start | bytes 294920 | tf_op jit(solution)/shard_map/ppermute | solution.py:20
  29.3 4.6 %collective-permute-start = (bf16[3,32,512]{2,0,1:T(4,128)(2,1)S(1)}, bf16[3,32,512]{2,0,1:T(4,128)(2,1)S(1)}, u32[]{:S(2)}, u32[]{:S(2)}) collective-permute-start(bf16[3,32,512]{2,0,1:T(4,128)(2,1)S(1)} %bitcast.87), channel_id=1, source_target_pairs={{0,2},{2,4},{4,6},{6,8},{8,10},{10,12},{12,14},{1,3},{3,5},{5,7},{... | collective-permute-start | bytes 294920 | tf_op jit(solution)/shard_map/ppermute | solution.py:18
  33.9 1.0 collective-permute-done.1
  34.9 2.9 %collective-permute-done = bf16[3,32,512]{2,0,1:T(4,128)(2,1)S(1)} collective-permute-done((bf16[3,32,512]{2,0,1:T(4,128)(2,1)S(1)}, bf16[3,32,512]{2,0,1:T(4,128)(2,1)S(1)}, u32[]{:S(2)}, u32[]{:S(2)}) %collective-permute-start) | collective-permute-done | bytes 98336 | tf_op jit(solution)/shard_map/ppermute | solution.py:18
  37.8 0.4 multiply_add_fusion
  38.6 5.1 %fusion.180 = (f32[3,32]{0,1:T(8,128)S(1)}, f32[3,32]{0,1:T(8,128)S(1)}, f32[3,32,512]{2,0,1:T(4,128)S(1)}) fusion(f32[512]{0:T(512)S(1)} %convert_element_type.101, f32[3]{0:T(128)} %get-tuple-element.67, f32[512]{0:T(512)S(1)} %bitcast.113, f32[9,38,512]{2,0,1:T(8,128)S(1)} %multiply_add_fusion, f32[512]{0:T(512)S(1)} %bitcast.111, f32[512]{0:T(512)S(1)} %bitcast.109, ...), kind=kLoop, calls=%fused_computation.312 | loop fusion | flops 5259072 | bytes 9933640 | tf_op jit(solution)/shard_map/reduce_sum | solution.py:106
  43.6 0.1 copy.28
  43.7 0.1 reduce_sum.41
  43.8 0.1 copy.29
  43.9 0.1 reduce_sum.43
  44.0 2.5 %all-reduce.3 = (f32[96]{0:T(128)S(1)}, f32[96]{0:T(128)S(1)}) all-reduce(f32[96]{0:T(128)S(1)} %reduce_sum.43, f32[96]{0:T(128)S(1)} %reduce_sum.41), channel_id=1, replica_groups=mesh['groups'=2,'rows'=8,'chan'=2] {'chan'}, use_global_device_ids=true, to_apply=%region_3.4 | all-reduce | flops 192 | bytes 1536 | tf_op jit(solution)/shard_map/psum | solution.py:106
  46.5 0.1 add_convert_fusion
  46.6 1.9 %all_gather.3 = bf16[96,1024]{1,0:T(8,128)(2,1)S(1)} all-gather(bf16[96,512]{1,0:T(8,128)(2,1)S(1)} %add_convert_fusion), channel_id=1, replica_groups=mesh['groups'=2,'rows'=8,'chan'=2] {'chan'}, dimensions={1}, use_global_device_ids=true | all-gather | bytes 294912 | tf_op jit(solution)/shard_map/all_gather | solution.py:114
  48.6 3.6 %fusion.7 = (bf16[96,2048]{1,0:T(8,128)(2,1)S(1)}, f32[96,2048]{1,0:T(8,128)S(1)}) fusion(f32[3,2048]{1,0:T(4,128)S(1)} %fusion.171, f32[2048]{0:T(1024)S(1)} %convert_element_type.105, bf16[96,1024]{1,0:T(8,128)(2,1)S(1)} %all_gather.3, bf16[1024,2048]{1,0:T(8,128)(2,1)} %param.23), kind=kOutput, calls=%fused_computation.56 | convolution fusion | flops 406585344 | bytes 5603328 | tf_op jit(solution)/shard_map/dot_general | solution.py:113
  52.2 2.1 %convolution_convert_fusion = bf16[96,1024]{1,0:T(8,128)(2,1)} fusion(bf16[96,2048]{1,0:T(8,128)(2,1)S(1)} %get-tuple-element.68, bf16[1024,2048]{1,0:T(8,128)(2,1)S(1)} %copy-done.1), kind=kOutput, calls=%fused_computation.49 | convolution fusion | flops 402751488 | bytes 4784128 | tf_op jit(solution)/shard_map/dot_general | solution.py:137
  54.3 0.1 fusion.165
  54.5 9.4 %reduce-scatter.5.cloned.1.call-done = bf16[96,512]{1,0:T(8,128)(2,1)} async-done(((bf16[96,1024]{1,0:T(8,128)(2,1)}), bf16[96,512]{1,0:T(8,128)(2,1)}) %reduce-scatter.5.cloned.1.call-update) | async-done | bytes 98320 | tf_op jit(solution)/shard_map/reduce_scatter | solution.py:140
  63.9 1.1 %fusion.162 = (f32[96]{0:T(128)S(1)}, f32[96]{0:T(128)S(1)}) fusion(bf16[96,512]{1,0:T(8,128)(2,1)} %reduce-scatter.5.cloned.1.call-done, f32[512]{0:T(512)S(1)} %convert_element_type.102, f32[96]{0:T(128)S(1)} %get-tuple-element.61, f32[96]{0:T(128)S(1)} %get-tuple-element.60, f32[3,32,512]{2,1,0:T(8,128)S(1)} %copy.27), kind=kLoop, calls=%fused_computation.275 | loop fusion | flops 343872 | bytes 298496 | tf_op jit(solution)/shard_map/reduce_sum | solution.py:144
  65.0 2.5 %all-reduce.2 = (f32[96]{0:T(128)S(1)}, f32[96]{0:T(128)S(1)}) all-reduce(f32[96]{0:T(128)S(1)} %get-tuple-element.5, f32[96]{0:T(128)S(1)} %get-tuple-element.4), channel_id=1, replica_groups=mesh['groups'=2,'rows'=8,'chan'=2] {'chan'}, use_global_device_ids=true, to_apply=%region_9.10 | all-reduce | flops 192 | bytes 1536 | tf_op jit(solution)/shard_map/psum | solution.py:144
  67.5 1.0 multiply_convert_fusion.2
  68.5 0.1 copy.30
  68.6 1.3 %collective-permute-start.3 = (bf16[3,32,512]{2,0,1:T(4,128)(2,1)S(1)}, bf16[3,32,512]{2,0,1:T(4,128)(2,1)S(1)}, u32[]{:S(2)}, u32[]{:S(2)}) collective-permute-start(bf16[3,32,512]{2,0,1:T(4,128)(2,1)S(1)} %copy.30), channel_id=1, source_target_pairs={{2,0},{4,2},{6,4},{8,6},{10,8},{12,10},{14,12},{3,1},{5,3},{7,5},{... | collective-permute-start | bytes 294920 | tf_op jit(solution)/shard_map/ppermute | solution.py:20
  69.9 4.6 %collective-permute-start.2 = (bf16[3,32,512]{2,0,1:T(4,128)(2,1)S(1)}, bf16[3,32,512]{2,0,1:T(4,128)(2,1)S(1)}, u32[]{:S(2)}, u32[]{:S(2)}) collective-permute-start(bf16[3,32,512]{2,0,1:T(4,128)(2,1)S(1)} %copy.30), channel_id=1, source_target_pairs={{0,2},{2,4},{4,6},{6,8},{8,10},{10,12},{12,14},{1,3},{3,5},{5,7},{... | collective-permute-start | bytes 294920 | tf_op jit(solution)/shard_map/ppermute | solution.py:18
  74.5 3.8 %fusion.13 = f32[96,1024]{1,0:T(8,128)} fusion(bf16[2048,1024]{1,0:T(8,128)(2,1)} %param.25, f32[96,2048]{1,0:T(8,128)S(1)} %get-tuple-element.69), kind=kOutput, calls=%fused_computation.64 | convolution fusion | flops 404422656 | bytes 5373952 | tf_op jit(solution)/shard_map/dot_general | solution.py:121
  78.7 0.5 collective-permute-done.2
  79.2 0.3 maximum_convert_fusion
  79.9 5.3 %add_add_fusion = f32[3,32,512]{2,0,1:T(4,128)} fusion(f32[9,32,512]{2,0,1:T(8,128)S(1)} %maximum_convert_fusion, f32[3,512]{1,0:T(4,128)S(1)} %fusion.165, f32[3]{0:T(128)} %get-tuple-element.67, f32[512]{0:T(512)S(1)} %bitcast.114, f32[512]{0:T(512)S(1)} %bitcast.112, f32[512]{0:T(512)S(1)} %bitcast.110, f32[512]{0:T(512)S(1)} %bitcast.108, ...), kind=kLoop, calls=%fused_computation.266 | loop fusion | flops 5111808 | bytes 3188808 | tf_op jit(solution)/shard_map/add | solution.py:150
  85.2 5.9 %all-to-all-start.1 = ((f32[3,32,512]{2,0,1:T(4,128)}), f32[3,32,512]{2,0,1:T(4,128)S(1)}, u32[]{:S(2)}, u32[]{:S(2)}) async-start(f32[3,32,512]{2,0,1:T(4,128)} %add_add_fusion), calls=%async_computation.3 | async-start | bytes 524288 | tf_op jit(solution)/shard_map/all_to_all | solution.py:222
  91.1 0.1 dynamic_slice.6
  91.2 0.7 convert_element_type.107
  92.1 1.6 %fusion.161 = bf16[96,512]{1,0:T(8,128)(2,1)} fusion(f32[3,32,512]{2,1,0:T(8,128)S(1)} %copy.26, f32[96,512]{1,0:T(8,128)} %reduce-scatter.3.cloned.1.call-done, f32[512]{0:T(512)S(1)} %convert_element_type.107, f32[512]{0:T(512)S(1)} %dynamic_slice.6), kind=kLoop, calls=%fused_computation.271 | loop fusion | flops 196608 | bytes 495616 | tf_op jit(solution)/shard_map/convert_element_type | solution.py:129
  93.7 6.3 %all-to-all-done.1 = f32[3,32,512]{2,0,1:T(4,128)S(1)} async-done(((f32[3,32,512]{2,0,1:T(4,128)}), f32[3,32,512]{2,0,1:T(4,128)S(1)}, u32[]{:S(2)}, u32[]{:S(2)}) %all-to-all-start.1) | async-done | bytes 196640 | tf_op jit(solution)/shard_map/all_to_all | solution.py:222
  99.9 0.8 copy.33
  (182 shorter events, 0.9 us)
Async XLA Ops:
  7.2 16.3 %copy-start.81 = (bf16[16,1024]{1,0:T(8,128)(2,1)S(1)}, bf16[16,1024]{1,0:T(8,128)(2,1)}, u32[]{:S(2)}) copy-start(bf16[16,1024]{1,0:T(8,128)(2,1)} %param.18) | copy-start | bytes 98308
  7.2 20.8 %all-to-all-start = ((bf16[24,4,512]{2,1,0:T(4,128)(2,1)}), bf16[24,4,512]{2,1,0:T(4,128)(2,1)S(1)}, u32[]{:S(2)}, u32[]{:S(2)}) async-start(bf16[24,4,512]{2,1,0:T(4,128)(2,1)} %param.14), calls=%async_computation | async-start | bytes 196608 | tf_op jit(solution)/shard_map/all_to_all | solution.py:188
  14.7 49.3 %reduce-scatter.5.cloned.1.call-start = ((), (), s32[]{:S(2)}) async-start(), calls=%async_computation.5 | async-start | bytes 294912 | tf_op jit(solution)/shard_map/reduce_scatter | solution.py:140
  15.7 22.5 %copy-start.2 = (f32[1,1,512]{2,1,0:T(1,128)}, f32[1,1,512]{2,1,0:T(1,128)S(1)}, u32[]{:S(2)}) copy-start(f32[1,1,512]{2,1,0:T(1,128)S(1)} %get-tuple-element.51) | copy-start | bytes 6148
  15.7 22.5 %copy-start.4 = (f32[1,1,512]{2,1,0:T(1,128)}, f32[1,1,512]{2,1,0:T(1,128)S(1)}, u32[]{:S(2)}) copy-start(f32[1,1,512]{2,1,0:T(1,128)S(1)} %get-tuple-element.52) | copy-start | bytes 6148
  15.7 22.5 %copy-start.6 = (f32[1,1,512]{2,1,0:T(1,128)}, f32[1,1,512]{2,1,0:T(1,128)S(1)}, u32[]{:S(2)}) copy-start(f32[1,1,512]{2,1,0:T(1,128)S(1)} %get-tuple-element.53) | copy-start | bytes 6148
  15.7 22.5 %copy-start.8 = (f32[1,1,512]{2,1,0:T(1,128)}, f32[1,1,512]{2,1,0:T(1,128)S(1)}, u32[]{:S(2)}) copy-start(f32[1,1,512]{2,1,0:T(1,128)S(1)} %get-tuple-element.54) | copy-start | bytes 6148
  15.7 22.5 %copy-start.10 = (f32[1,1,512]{2,1,0:T(1,128)}, f32[1,1,512]{2,1,0:T(1,128)S(1)}, u32[]{:S(2)}) copy-start(f32[1,1,512]{2,1,0:T(1,128)S(1)} %get-tuple-element.55) | copy-start | bytes 6148
  15.7 22.5 %copy-start.12 = (f32[1,1,512]{2,1,0:T(1,128)}, f32[1,1,512]{2,1,0:T(1,128)S(1)}, u32[]{:S(2)}) copy-start(f32[1,1,512]{2,1,0:T(1,128)S(1)} %get-tuple-element.56) | copy-start | bytes 6148
  15.7 22.5 %copy-start.14 = (f32[1,1,512]{2,1,0:T(1,128)}, f32[1,1,512]{2,1,0:T(1,128)S(1)}, u32[]{:S(2)}) copy-start(f32[1,1,512]{2,1,0:T(1,128)S(1)} %get-tuple-element.57) | copy-start | bytes 6148
  15.8 22.5 %copy-start.16 = (f32[1,1,512]{2,1,0:T(1,128)}, f32[1,1,512]{2,1,0:T(1,128)S(1)}, u32[]{:S(2)}) copy-start(f32[1,1,512]{2,1,0:T(1,128)S(1)} %get-tuple-element.58) | copy-start | bytes 6148
  15.8 22.5 %copy-start.18 = (f32[1,1,512]{2,1,0:T(1,128)}, f32[1,1,512]{2,1,0:T(1,128)S(1)}, u32[]{:S(2)}) copy-start(f32[1,1,512]{2,1,0:T(1,128)S(1)} %get-tuple-element.59) | copy-start | bytes 6148
  16.9 21.3 %copy-start.20 = (f32[1,1,512]{2,1,0:T(1,128)}, f32[1,1,512]{2,1,0:T(1,128)S(1)}, u32[]{:S(2)}) copy-start(f32[1,1,512]{2,1,0:T(1,128)S(1)} %get-tuple-element.30) | copy-start | bytes 6148
  16.9 21.3 %copy-start.22 = (f32[1,1,512]{2,1,0:T(1,128)}, f32[1,1,512]{2,1,0:T(1,128)S(1)}, u32[]{:S(2)}) copy-start(f32[1,1,512]{2,1,0:T(1,128)S(1)} %get-tuple-element.31) | copy-start | bytes 6148
  16.9 21.3 %copy-start.24 = (f32[1,1,512]{2,1,0:T(1,128)}, f32[1,1,512]{2,1,0:T(1,128)S(1)}, u32[]{:S(2)}) copy-start(f32[1,1,512]{2,1,0:T(1,128)S(1)} %get-tuple-element.32) | copy-start | bytes 6148
  16.9 21.3 %copy-start.26 = (f32[1,1,512]{2,1,0:T(1,128)}, f32[1,1,512]{2,1,0:T(1,128)S(1)}, u32[]{:S(2)}) copy-start(f32[1,1,512]{2,1,0:T(1,128)S(1)} %get-tuple-element.33) | copy-start | bytes 6148
  17.0 21.3 %copy-start.28 = (f32[1,1,512]{2,1,0:T(1,128)}, f32[1,1,512]{2,1,0:T(1,128)S(1)}, u32[]{:S(2)}) copy-start(f32[1,1,512]{2,1,0:T(1,128)S(1)} %get-tuple-element.34) | copy-start | bytes 6148
  17.0 21.3 %copy-start.30 = (f32[1,1,512]{2,1,0:T(1,128)}, f32[1,1,512]{2,1,0:T(1,128)S(1)}, u32[]{:S(2)}) copy-start(f32[1,1,512]{2,1,0:T(1,128)S(1)} %get-tuple-element.35) | copy-start | bytes 6148
  17.0 21.3 %copy-start.32 = (f32[1,1,512]{2,1,0:T(1,128)}, f32[1,1,512]{2,1,0:T(1,128)S(1)}, u32[]{:S(2)}) copy-start(f32[1,1,512]{2,1,0:T(1,128)S(1)} %get-tuple-element.36) | copy-start | bytes 6148
  17.0 21.3 %copy-start.34 = (f32[1,1,512]{2,1,0:T(1,128)}, f32[1,1,512]{2,1,0:T(1,128)S(1)}, u32[]{:S(2)}) copy-start(f32[1,1,512]{2,1,0:T(1,128)S(1)} %get-tuple-element.37) | copy-start | bytes 6148
  17.0 21.3 %copy-start.36 = (f32[1,1,512]{2,1,0:T(1,128)}, f32[1,1,512]{2,1,0:T(1,128)S(1)}, u32[]{:S(2)}) copy-start(f32[1,1,512]{2,1,0:T(1,128)S(1)} %get-tuple-element.38) | copy-start | bytes 6148
  17.0 21.3 %copy-start.38 = (f32[1,1,512]{2,1,0:T(1,128)}, f32[1,1,512]{2,1,0:T(1,128)S(1)}, u32[]{:S(2)}) copy-start(f32[1,1,512]{2,1,0:T(1,128)S(1)} %get-tuple-element.39) | copy-start | bytes 6148
  17.0 21.3 %copy-start.40 = (f32[1,1,512]{2,1,0:T(1,128)}, f32[1,1,512]{2,1,0:T(1,128)S(1)}, u32[]{:S(2)}) copy-start(f32[1,1,512]{2,1,0:T(1,128)S(1)} %get-tuple-element.40) | copy-start | bytes 6148
  17.0 21.3 %copy-start.42 = (f32[1,1,512]{2,1,0:T(1,128)}, f32[1,1,512]{2,1,0:T(1,128)S(1)}, u32[]{:S(2)}) copy-start(f32[1,1,512]{2,1,0:T(1,128)S(1)} %get-tuple-element.41) | copy-start | bytes 6148
  17.0 21.3 %copy-start.44 = (f32[1,1,512]{2,1,0:T(1,128)}, f32[1,1,512]{2,1,0:T(1,128)S(1)}, u32[]{:S(2)}) copy-start(f32[1,1,512]{2,1,0:T(1,128)S(1)} %get-tuple-element.42) | copy-start | bytes 6148
  17.0 21.3 %copy-start.46 = (f32[1,1,512]{2,1,0:T(1,128)}, f32[1,1,512]{2,1,0:T(1,128)S(1)}, u32[]{:S(2)}) copy-start(f32[1,1,512]{2,1,0:T(1,128)S(1)} %get-tuple-element.43) | copy-start | bytes 6148
  17.1 21.3 %copy-start.48 = (f32[1,1,512]{2,1,0:T(1,128)}, f32[1,1,512]{2,1,0:T(1,128)S(1)}, u32[]{:S(2)}) copy-start(f32[1,1,512]{2,1,0:T(1,128)S(1)} %get-tuple-element.44) | copy-start | bytes 6148
  17.1 21.3 %copy-start.50 = (f32[1,1,512]{2,1,0:T(1,128)}, f32[1,1,512]{2,1,0:T(1,128)S(1)}, u32[]{:S(2)}) copy-start(f32[1,1,512]{2,1,0:T(1,128)S(1)} %get-tuple-element.45) | copy-start | bytes 6148
  17.1 21.3 %copy-start.52 = (f32[1,1,512]{2,1,0:T(1,128)}, f32[1,1,512]{2,1,0:T(1,128)S(1)}, u32[]{:S(2)}) copy-start(f32[1,1,512]{2,1,0:T(1,128)S(1)} %get-tuple-element.46) | copy-start | bytes 6148
  17.1 21.3 %copy-start.54 = (f32[1,1,512]{2,1,0:T(1,128)}, f32[1,1,512]{2,1,0:T(1,128)S(1)}, u32[]{:S(2)}) copy-start(f32[1,1,512]{2,1,0:T(1,128)S(1)} %get-tuple-element.47) | copy-start | bytes 6148
  17.1 21.3 %copy-start.56 = (f32[1,1,512]{2,1,0:T(1,128)}, f32[1,1,512]{2,1,0:T(1,128)S(1)}, u32[]{:S(2)}) copy-start(f32[1,1,512]{2,1,0:T(1,128)S(1)} %get-tuple-element.48) | copy-start | bytes 6148
  18.7 19.7 %copy-start.58 = (f32[1,1,512]{2,1,0:T(1,128)}, f32[1,1,512]{2,1,0:T(1,128)S(1)}, u32[]{:S(2)}) copy-start(f32[1,1,512]{2,1,0:T(1,128)S(1)} %get-tuple-element.11) | copy-start | bytes 6148
  18.8 19.7 %copy-start.60 = (f32[1,1,512]{2,1,0:T(1,128)}, f32[1,1,512]{2,1,0:T(1,128)S(1)}, u32[]{:S(2)}) copy-start(f32[1,1,512]{2,1,0:T(1,128)S(1)} %get-tuple-element.12) | copy-start | bytes 6148
  18.8 19.7 %copy-start.62 = (f32[1,1,512]{2,1,0:T(1,128)}, f32[1,1,512]{2,1,0:T(1,128)S(1)}, u32[]{:S(2)}) copy-start(f32[1,1,512]{2,1,0:T(1,128)S(1)} %get-tuple-element.13) | copy-start | bytes 6148
  18.8 19.7 %copy-start.64 = (f32[1,1,512]{2,1,0:T(1,128)}, f32[1,1,512]{2,1,0:T(1,128)S(1)}, u32[]{:S(2)}) copy-start(f32[1,1,512]{2,1,0:T(1,128)S(1)} %get-tuple-element.14) | copy-start | bytes 6148
  18.8 19.7 %copy-start.66 = (f32[1,1,512]{2,1,0:T(1,128)}, f32[1,1,512]{2,1,0:T(1,128)S(1)}, u32[]{:S(2)}) copy-start(f32[1,1,512]{2,1,0:T(1,128)S(1)} %get-tuple-element.15) | copy-start | bytes 6148
  18.8 19.7 %copy-start.68 = (f32[1,1,512]{2,1,0:T(1,128)}, f32[1,1,512]{2,1,0:T(1,128)S(1)}, u32[]{:S(2)}) copy-start(f32[1,1,512]{2,1,0:T(1,128)S(1)} %get-tuple-element.16) | copy-start | bytes 6148
  18.8 19.7 %copy-start.70 = (f32[1,1,512]{2,1,0:T(1,128)}, f32[1,1,512]{2,1,0:T(1,128)S(1)}, u32[]{:S(2)}) copy-start(f32[1,1,512]{2,1,0:T(1,128)S(1)} %get-tuple-element.17) | copy-start | bytes 6148
  18.8 19.7 %copy-start.72 = (f32[1,1,512]{2,1,0:T(1,128)}, f32[1,1,512]{2,1,0:T(1,128)S(1)}, u32[]{:S(2)}) copy-start(f32[1,1,512]{2,1,0:T(1,128)S(1)} %get-tuple-element.18) | copy-start | bytes 6148
  18.8 19.7 %copy-start.74 = (f32[1,1,512]{2,1,0:T(1,128)}, f32[1,1,512]{2,1,0:T(1,128)S(1)}, u32[]{:S(2)}) copy-start(f32[1,1,512]{2,1,0:T(1,128)S(1)} %get-tuple-element.19) | copy-start | bytes 6148
  18.8 19.7 %copy-start.76 = (f32[1,1,512]{2,1,0:T(1,128)}, f32[1,1,512]{2,1,0:T(1,128)S(1)}, u32[]{:S(2)}) copy-start(f32[1,1,512]{2,1,0:T(1,128)S(1)} %get-tuple-element.20) | copy-start | bytes 6148
  18.8 19.7 %copy-start.78 = (f32[1,1,512]{2,1,0:T(1,128)}, f32[1,1,512]{2,1,0:T(1,128)S(1)}, u32[]{:S(2)}) copy-start(f32[1,1,512]{2,1,0:T(1,128)S(1)} %get-tuple-element.21) | copy-start | bytes 6148
  28.0 6.9 %collective-permute-start.1 = (bf16[3,32,512]{2,0,1:T(4,128)(2,1)S(1)}, bf16[3,32,512]{2,0,1:T(4,128)(2,1)S(1)}, u32[]{:S(2)}, u32[]{:S(2)}) collective-permute-start(bf16[3,32,512]{2,0,1:T(4,128)(2,1)S(1)} %bitcast.86), channel_id=1, source_target_pairs={{2,0},{4,2},{6,4},{8,6},{10,8},{12,10},{14,12},{3,1},{5,3},{7,5},{... | collective-permute-start | bytes 294920 | tf_op jit(solution)/shard_map/ppermute | solution.py:20
  29.3 8.5 %collective-permute-start = (bf16[3,32,512]{2,0,1:T(4,128)(2,1)S(1)}, bf16[3,32,512]{2,0,1:T(4,128)(2,1)S(1)}, u32[]{:S(2)}, u32[]{:S(2)}) collective-permute-start(bf16[3,32,512]{2,0,1:T(4,128)(2,1)S(1)} %bitcast.87), channel_id=1, source_target_pairs={{0,2},{2,4},{4,6},{6,8},{8,10},{10,12},{12,14},{1,3},{3,5},{5,7},{... | collective-permute-start | bytes 294920 | tf_op jit(solution)/shard_map/ppermute | solution.py:18
  54.3 37.8 %reduce-scatter.3.cloned.1.call-start = ((), (), s32[]{:S(2)}) async-start(), calls=%async_computation.4 | async-start | bytes 589824 | tf_op jit(solution)/shard_map/reduce_scatter | solution.py:120
  68.6 10.1 %collective-permute-start.3 = (bf16[3,32,512]{2,0,1:T(4,128)(2,1)S(1)}, bf16[3,32,512]{2,0,1:T(4,128)(2,1)S(1)}, u32[]{:S(2)}, u32[]{:S(2)}) collective-permute-start(bf16[3,32,512]{2,0,1:T(4,128)(2,1)S(1)} %copy.30), channel_id=1, source_target_pairs={{2,0},{4,2},{6,4},{8,6},{10,8},{12,10},{14,12},{3,1},{5,3},{7,5},{... | collective-permute-start | bytes 294920 | tf_op jit(solution)/shard_map/ppermute | solution.py:20
  69.9 9.3 %collective-permute-start.2 = (bf16[3,32,512]{2,0,1:T(4,128)(2,1)S(1)}, bf16[3,32,512]{2,0,1:T(4,128)(2,1)S(1)}, u32[]{:S(2)}, u32[]{:S(2)}) collective-permute-start(bf16[3,32,512]{2,0,1:T(4,128)(2,1)S(1)} %copy.30), channel_id=1, source_target_pairs={{0,2},{2,4},{4,6},{6,8},{8,10},{10,12},{12,14},{1,3},{3,5},{5,7},{... | collective-permute-start | bytes 294920 | tf_op jit(solution)/shard_map/ppermute | solution.py:18
  85.2 14.7 %all-to-all-start.1 = ((f32[3,32,512]{2,0,1:T(4,128)}), f32[3,32,512]{2,0,1:T(4,128)S(1)}, u32[]{:S(2)}, u32[]{:S(2)}) async-start(f32[3,32,512]{2,0,1:T(4,128)} %add_add_fusion), calls=%async_computation.3 | async-start | bytes 524288 | tf_op jit(solution)/shard_map/all_to_all | solution.py:222
  (43 other events, 93.4 us)
Sparse Core Ops, SparseCore 0:
  54.4 9.4 reduce-scatter.4
  78.8 8.9 reduce-scatter.2
where the time goes:
time: 109 us; the launch traced here: 108 us
  starting transfers between devices  25.1 us (23%)
  waiting for transfers between devices  20.2 us (19%)
  other arithmetic  19.8 us (18%)
  between operations  15.5 us (14%)
  matrix products  14.5 us (13%)
  blocking collectives  6.89 us (6%)
  local copies, waits for them, and re-layouts  5.62 us (5%)
    reduce_scatter x1, waiting for transfers between devices, local_block(): lax.psum_scatter(grad_terms.astype(jnp.bfloat16), 'chan', scatter_dimensi...  9.45 us
    ppermute x2, starting transfers between devices, with_halo(): lax.ppermute(tail, axis, [(i, (i + 1) % count) for i in range(ends)])  9.11 us
    all_to_all x1, starting transfers between devices, per_device(): lax.all_to_all(latents, 'rows', split_axis=0, concat_axis=1, tiled=True)  7.45 us
    all_to_all x1, waiting for transfers between devices, per_device(): lax.all_to_all(gradient, 'rows', split_axis=1, concat_axis=0, tiled=True)  6.28 us
    all_to_all x1, starting transfers between devices, per_device(): lax.all_to_all(gradient, 'rows', split_axis=1, concat_axis=0, tiled=True)  5.88 us
    add x1, other arithmetic, local_block(): stencil(grad_pad, kernel[::-1, ::-1], masks) + class_tokens[:, None, :]  5.34 us
    reduce_sum x1, other arithmetic, local_block(): jnp.sum(flat, 1)  5.05 us
    dot_general x1, matrix products, local_block(): jnp.dot(active, down_weight, preferred_element_type=jnp.float32)  3.82 us
  transfers between devices with their start and end apart: 8, of which 5 were waited for; matrix products, arithmetic and copies ran while one was open for 23% of the time, Pallas kernels for 0%

commit v1 on v0

--- a/solution.py
+++ b/solution.py
@@ -5,6 +5,24 @@
 
 KAPPA = 0.7978845608028654
 EPSILON = 1e-06
+
+
+def deliver_the_matrix(here_x):
+    val, extra = (lax.axis_size("rows"), lax.axis_index("rows"))
+    m_next = here_x.shape[0] // val
+    x_next = list(here_x.shape)
+    x_next[0] = m_next
+    e_next = x_next[1]
+    x_next[1] = e_next * val
+    latest = jnp.zeros(x_next, here_x.dtype)
+    for k0 in range(val):
+        work_now = lax.dynamic_slice_in_dim(here_x, (extra ^ k0) * m_next, m_next, axis=0)
+        if k0:
+            work_now = lax.ppermute(
+                work_now, axis_name="rows", perm=[(num, num ^ k0) for num in range(val)]
+            )
+        latest = lax.dynamic_update_slice_in_dim(latest, work_now, (extra ^ k0) * e_next, axis=1)
+    return latest
 
 
 def with_halo(cells, sides, width):
@@ -185,7 +203,7 @@
     slope_image = lax.dot_general(
         direction, down_weight, (((1,), (1,)), ((), ())), preferred_element_type=jnp.float32
     )
-    latent_rows = lax.all_to_all(latents, "rows", split_axis=0, concat_axis=1, tiled=True)
+    latent_rows = deliver_the_matrix(latents)
     height = latent_rows.shape[0]
     width = latent_rows.shape[1]
     row_first = lax.axis_index("rows") * height

time: 109 us -> 117 us (1.073)
  starting transfers between devices: 25.1 us -> 30.7 us
  other arithmetic: 19.8 us -> 17.5 us
  waiting for transfers between devices: 20.2 us -> 22.5 us
  matrix products: 14.5 us -> 15.9 us
    ppermute x0 -> x7, starting transfers between devices: none -> 12.9 us  [deliver_the_matrix(): lax.ppermute(work_now, axis_name='rows', perm=[(num, num ^ k0) for num in...]
    all_to_all x1 -> x0, starting transfers between devices: 7.45 us -> none  [per_device(): lax.all_to_all(latents, 'rows', split_axis=0, concat_axis=1, tiled=True)]
    ppermute x0 -> x7, waiting for transfers between devices: none -> 6.3 us  [deliver_the_matrix(): lax.ppermute(work_now, axis_name='rows', perm=[(num, num ^ k0) for num in...]
    reduce_scatter x1, waiting for transfers between devices: 9.45 us -> 7.03 us  [local_block(): lax.psum_scatter(grad_terms.astype(jnp.bfloat16), 'chan', scatter_dimensi...]
    ppermute x2, waiting for transfers between devices: 3.39 us -> 1.82 us  [with_halo(): lax.ppermute(tail, axis, [(i, (i + 1) % count) for i in range(ends)])]
    dot_general x5, matrix products: 1.62 us -> 2.98 us  [exact_dot(): jnp.dot(left, right, precision=lax.Precision.HIGHEST, preferred_element_t...]
  transfers between devices with their start and end apart: 8 -> 14, of which waited for: 5 -> 7; matrix products, arithmetic and copies ran while one was open for 23% -> 21% of each run, Pallas kernels for 0% -> 0%
where the time goes in v1:
time: 117 us; the launch traced here: 116 us
  starting transfers between devices  30.7 us (26%)
  waiting for transfers between devices  22.5 us (19%)
  other arithmetic  17.5 us (15%)
  matrix products  15.9 us (14%)
  between operations  15.7 us (13%)
  blocking collectives  6.89 us (6%)
  local copies, waits for them, and re-layouts  6.71 us (6%)
    ppermute x7, starting transfers between devices, deliver_the_matrix(): lax.ppermute(work_now, axis_name='rows', perm=[(num, num ^ k0) for num in...  12.9 us
    ppermute x2, starting transfers between devices, with_halo(): lax.ppermute(tail, axis, [(i, (i + 1) % count) for i in range(ends)])  9.29 us
    reduce_scatter x1, waiting for transfers between devices, local_block(): lax.psum_scatter(grad_terms.astype(jnp.bfloat16), 'chan', scatter_dimensi...  7.03 us
    ppermute x7, waiting for transfers between devices, deliver_the_matrix(): lax.ppermute(work_now, axis_name='rows', perm=[(num, num ^ k0) for num in...  6.3 us
    all_to_all x1, waiting for transfers between devices, per_device(): lax.all_to_all(gradient, 'rows', split_axis=1, concat_axis=0, tiled=True)  6.28 us
    all_to_all x1, starting transfers between devices, per_device(): lax.all_to_all(gradient, 'rows', split_axis=1, concat_axis=0, tiled=True)  5.89 us
    add x1, other arithmetic, local_block(): stencil(grad_pad, kernel[::-1, ::-1], masks) + class_tokens[:, None, :]  5.27 us
    reduce_sum x1, other arithmetic, local_block(): jnp.sum(flat, 1)  5.01 us
  transfers between devices with their start and end apart: 14, of which 7 were waited for; matrix products, arithmetic and copies ran while one was open for 21% of the time, Pallas kernels for 0%

profile of v1, /device:TPU:0, one launch (start us, length us, event | category | flops | bytes accessed | tf_op | source)
XLA Modules:
  0.0 115.9 jit_solution(4038298779071343087)
XLA Ops:
  7.3 0.9 constant_dynamic-slice_fusion
  8.2 3.1 %collective-permute-start = (bf16[3,4,512]{2,0,1:T(4,128)(2,1)S(1)}, bf16[3,4,512]{2,0,1:T(4,128)(2,1)S(1)}, u32[]{:S(2)}, u32[]{:S(2)}) collective-permute-start(bf16[3,4,512]{2,0,1:T(4,128)(2,1)S(1)} %copy.48), channel_id=1, source_target_pairs={{0,2},{2,0},{4,6},{6,4},{8,10},{10,8},{12,14},{14,12},{1,3},{3,1},... | collective-permute-start | bytes 36872 | tf_op jit(solution)/shard_map/ppermute | solution.py:21
  11.3 1.6 %collective-permute-start.1 = (bf16[3,4,512]{2,0,1:T(4,128)(2,1)S(1)}, bf16[3,4,512]{2,0,1:T(4,128)(2,1)S(1)}, u32[]{:S(2)}, u32[]{:S(2)}) collective-permute-start(bf16[3,4,512]{2,0,1:T(4,128)(2,1)S(1)} %copy.49), channel_id=1, source_target_pairs={{0,4},{2,6},{4,0},{6,2},{8,12},{10,14},{12,8},{14,10},{1,5},{3,7},... | collective-permute-start | bytes 36872 | tf_op jit(solution)/shard_map/ppermute | solution.py:21
  13.0 3.0 %collective-permute-start.3 = (bf16[3,4,512]{2,0,1:T(4,128)(2,1)S(1)}, bf16[3,4,512]{2,0,1:T(4,128)(2,1)S(1)}, u32[]{:S(2)}, u32[]{:S(2)}) collective-permute-start(bf16[3,4,512]{2,0,1:T(4,128)(2,1)S(1)} %copy.51), channel_id=1, source_target_pairs={{0,8},{2,10},{4,12},{6,14},{8,0},{10,2},{12,4},{14,6},{1,9},{3,11}... | collective-permute-start | bytes 36872 | tf_op jit(solution)/shard_map/ppermute | solution.py:21
  16.1 1.4 %collective-permute-start.4 = (bf16[3,4,512]{2,0,1:T(4,128)(2,1)S(1)}, bf16[3,4,512]{2,0,1:T(4,128)(2,1)S(1)}, u32[]{:S(2)}, u32[]{:S(2)}) collective-permute-start(bf16[3,4,512]{2,0,1:T(4,128)(2,1)S(1)} %copy.52), channel_id=1, source_target_pairs={{0,10},{2,8},{4,14},{6,12},{8,2},{10,0},{12,6},{14,4},{1,11},{3,9}... | collective-permute-start | bytes 36872 | tf_op jit(solution)/shard_map/ppermute | solution.py:21
  17.4 1.0 fusion.184
  18.4 1.1 fusion.183
  19.8 1.6 %fusion.182 = (f32[1,1,512]{2,1,0:T(1,128)S(1)}, f32[1,1,512]{2,1,0:T(1,128)S(1)}, f32[1,1,512]{2,1,0:T(1,128)S(1)}, f32[1,1,512]{2,1,0:T(1,128)S(1)}, f32[1,1,5...) fusion(bf16[7,7,512]{2,1,0:T(8,128)(2,1)} %param.19), kind=kLoop, calls=%fused_computation.329 | loop fusion | bytes 77824 | tf_op jit(solution)/shard_map/slice | solution.py:67
  21.6 0.7 iota_compare_fusion.4
  22.2 0.7 convert_element_type.93
  22.9 0.9 fusion.163
  23.9 0.2 fusion.179
  24.1 0.2 fusion.170
  24.3 3.4 %fusion.164 = f32[3,2048]{1,0:T(4,128)S(1)} fusion(bf16[2048,1024]{1,0:T(8,128)(2,1)} %param.25, f32[3,1024]{1,0:T(4,128)S(1)} %fusion.170, f32[1024]{0:T(1024)S(1)} %convert_element_type.93), kind=kOutput, calls=%fused_computation.281 | convolution fusion | flops 12589056 | bytes 4235264 | tf_op jit(solution)/shard_map/dot_general | solution.py:203
  27.7 0.8 fusion.172
  28.6 0.7 compare_convert_fusion.5
  29.4 3.7 %collective-permute-start.5 = (bf16[3,4,512]{2,0,1:T(4,128)(2,1)S(1)}, bf16[3,4,512]{2,0,1:T(4,128)(2,1)S(1)}, u32[]{:S(2)}, u32[]{:S(2)}) collective-permute-start(bf16[3,4,512]{2,0,1:T(4,128)(2,1)S(1)} %copy.53), channel_id=1, source_target_pairs={{0,12},{2,14},{4,8},{6,10},{8,4},{10,6},{12,0},{14,2},{1,13},{3,15... | collective-permute-start | bytes 36872 | tf_op jit(solution)/shard_map/ppermute | solution.py:21
  33.3 1.7 %collective-permute-done.5 = bf16[3,4,512]{2,0,1:T(4,128)(2,1)S(1)} collective-permute-done((bf16[3,4,512]{2,0,1:T(4,128)(2,1)S(1)}, bf16[3,4,512]{2,0,1:T(4,128)(2,1)S(1)}, u32[]{:S(2)}, u32[]{:S(2)}) %collective-permute-start.5) | collective-permute-done | bytes 12320 | tf_op jit(solution)/shard_map/ppermute | solution.py:21
  35.1 4.6 %collective-permute-done.6 = bf16[3,4,512]{2,0,1:T(4,128)(2,1)S(1)} collective-permute-done((bf16[3,4,512]{2,0,1:T(4,128)(2,1)S(1)}, bf16[3,4,512]{2,0,1:T(4,128)(2,1)S(1)}, u32[]{:S(2)}, u32[]{:S(2)}) %collective-permute-start.6) | collective-permute-done | bytes 12320 | tf_op jit(solution)/shard_map/ppermute | solution.py:21
  39.6 1.3 %collective-permute-start.8 = (bf16[3,32,512]{2,0,1:T(4,128)(2,1)S(1)}, bf16[3,32,512]{2,0,1:T(4,128)(2,1)S(1)}, u32[]{:S(2)}, u32[]{:S(2)}) collective-permute-start(bf16[3,32,512]{2,0,1:T(4,128)(2,1)S(1)} %constant_dynamic-update-slice_fusion), channel_id=1, source_target_pairs={{2,0},{4,2},{6,4},{8,6},{10,8},{12,10},{14,12},{3,1},{5,3},{7,5},{... | collective-permute-start | bytes 294920 | tf_op jit(solution)/shard_map/ppermute | solution.py:38
  40.9 4.6 %collective-permute-start.7 = (bf16[3,32,512]{2,0,1:T(4,128)(2,1)S(1)}, bf16[3,32,512]{2,0,1:T(4,128)(2,1)S(1)}, u32[]{:S(2)}, u32[]{:S(2)}) collective-permute-start(bf16[3,32,512]{2,0,1:T(4,128)(2,1)S(1)} %constant_dynamic-update-slice_fusion), channel_id=1, source_target_pairs={{0,2},{2,4},{4,6},{6,8},{8,10},{10,12},{12,14},{1,3},{3,5},{5,7},{... | collective-permute-start | bytes 294920 | tf_op jit(solution)/shard_map/ppermute | solution.py:36
  45.5 1.0 collective-permute-done.8
  46.5 1.5 %collective-permute-done.7 = bf16[3,32,512]{2,0,1:T(4,128)(2,1)S(1)} collective-permute-done((bf16[3,32,512]{2,0,1:T(4,128)(2,1)S(1)}, bf16[3,32,512]{2,0,1:T(4,128)(2,1)S(1)}, u32[]{:S(2)}, u32[]{:S(2)}) %collective-permute-start.7) | collective-permute-done | bytes 98336 | tf_op jit(solution)/shard_map/ppermute | solution.py:36
  48.0 0.4 multiply_add_fusion
  48.8 5.0 %fusion.180 = (f32[3,32]{0,1:T(8,128)S(1)}, f32[3,32]{0,1:T(8,128)S(1)}, f32[3,32,512]{2,0,1:T(4,128)S(1)}) fusion(f32[512]{0:T(512)S(1)} %convert_element_type.101, f32[3]{0:T(128)} %get-tuple-element.75, f32[512]{0:T(512)S(1)} %bitcast.105, f32[9,38,512]{2,0,1:T(8,128)S(1)} %multiply_add_fusion, f32[512]{0:T(512)S(1)} %bitcast.103, f32[512]{0:T(512)S(1)} %bitcast.101, ...), kind=kLoop, calls=%fused_computation.328 | loop fusion | flops 5259072 | bytes 9933640 | tf_op jit(solution)/shard_map/reduce_sum | solution.py:124
  53.9 0.1 reduce_sum.41
  54.2 2.5 %all-reduce.3 = (f32[96]{0:T(128)S(1)}, f32[96]{0:T(128)S(1)}) all-reduce(f32[96]{0:T(128)S(1)} %reduce_sum.43, f32[96]{0:T(128)S(1)} %reduce_sum.41), channel_id=1, replica_groups=mesh['groups'=2,'rows'=8,'chan'=2] {'chan'}, use_global_device_ids=true, to_apply=%region_3.4 | all-reduce | flops 192 | bytes 1536 | tf_op jit(solution)/shard_map/psum | solution.py:124
  56.7 0.1 add_convert_fusion
  56.8 1.9 %all_gather.3 = bf16[96,1024]{1,0:T(8,128)(2,1)S(1)} all-gather(bf16[96,512]{1,0:T(8,128)(2,1)S(1)} %add_convert_fusion), channel_id=1, replica_groups=mesh['groups'=2,'rows'=8,'chan'=2] {'chan'}, dimensions={1}, use_global_device_ids=true | all-gather | bytes 294912 | tf_op jit(solution)/shard_map/all_gather | solution.py:132
  58.7 3.6 %fusion.7 = (bf16[96,2048]{1,0:T(8,128)(2,1)S(1)}, f32[96,2048]{1,0:T(8,128)S(1)}) fusion(f32[3,2048]{1,0:T(4,128)S(1)} %fusion.172, f32[2048]{0:T(1024)S(1)} %convert_element_type.105, bf16[96,1024]{1,0:T(8,128)(2,1)S(1)} %all_gather.3, bf16[1024,2048]{1,0:T(8,128)(2,1)} %param.23), kind=kOutput, calls=%fused_computation.56 | convolution fusion | flops 406585344 | bytes 5603328 | tf_op jit(solution)/shard_map/dot_general | solution.py:131
  62.3 2.1 %convolution_convert_fusion = bf16[96,1024]{1,0:T(8,128)(2,1)} fusion(bf16[96,2048]{1,0:T(8,128)(2,1)S(1)} %get-tuple-element.76, bf16[1024,2048]{1,0:T(8,128)(2,1)S(1)} %copy-done.1), kind=kOutput, calls=%fused_computation.49 | convolution fusion | flops 402751488 | bytes 4784128 | tf_op jit(solution)/shard_map/dot_general | solution.py:155
  64.5 0.8 fusion.165
  65.3 7.0 %reduce-scatter.5.cloned.1.call-done = bf16[96,512]{1,0:T(8,128)(2,1)} async-done(((bf16[96,1024]{1,0:T(8,128)(2,1)}), bf16[96,512]{1,0:T(8,128)(2,1)}) %reduce-scatter.5.cloned.1.call-update) | async-done | bytes 98320 | tf_op jit(solution)/shard_map/reduce_scatter | solution.py:158
  72.4 1.1 fusion.162
  73.5 2.5 %all-reduce.2 = (f32[96]{0:T(128)S(1)}, f32[96]{0:T(128)S(1)}) all-reduce(f32[96]{0:T(128)S(1)} %get-tuple-element.5, f32[96]{0:T(128)S(1)} %get-tuple-element.4), channel_id=1, replica_groups=mesh['groups'=2,'rows'=8,'chan'=2] {'chan'}, use_global_device_ids=true, to_apply=%region_9.10 | all-reduce | flops 192 | bytes 1536 | tf_op jit(solution)/shard_map/psum | solution.py:162
  76.0 1.0 multiply_convert_fusion.2
  77.0 0.1 copy.43
  77.1 1.3 %collective-permute-start.10 = (bf16[3,32,512]{2,0,1:T(4,128)(2,1)S(1)}, bf16[3,32,512]{2,0,1:T(4,128)(2,1)S(1)}, u32[]{:S(2)}, u32[]{:S(2)}) collective-permute-start(bf16[3,32,512]{2,0,1:T(4,128)(2,1)S(1)} %copy.43), channel_id=1, source_target_pairs={{2,0},{4,2},{6,4},{8,6},{10,8},{12,10},{14,12},{3,1},{5,3},{7,5},{... | collective-permute-start | bytes 294920 | tf_op jit(solution)/shard_map/ppermute | solution.py:38
  78.4 4.7 %collective-permute-start.9 = (bf16[3,32,512]{2,0,1:T(4,128)(2,1)S(1)}, bf16[3,32,512]{2,0,1:T(4,128)(2,1)S(1)}, u32[]{:S(2)}, u32[]{:S(2)}) collective-permute-start(bf16[3,32,512]{2,0,1:T(4,128)(2,1)S(1)} %copy.43), channel_id=1, source_target_pairs={{0,2},{2,4},{4,6},{6,8},{8,10},{10,12},{12,14},{1,3},{3,5},{5,7},{... | collective-permute-start | bytes 294920 | tf_op jit(solution)/shard_map/ppermute | solution.py:36
  83.1 3.8 %fusion.13 = f32[96,1024]{1,0:T(8,128)} fusion(bf16[2048,1024]{1,0:T(8,128)(2,1)} %param.25, f32[96,2048]{1,0:T(8,128)S(1)} %get-tuple-element.77), kind=kOutput, calls=%fused_computation.64 | convolution fusion | flops 404422656 | bytes 5373952 | tf_op jit(solution)/shard_map/dot_general | solution.py:139
  87.3 0.3 collective-permute-done.9
  87.6 0.3 maximum_convert_fusion
  88.3 5.3 %add_add_fusion = f32[3,32,512]{2,0,1:T(4,128)} fusion(f32[9,32,512]{2,0,1:T(8,128)S(1)} %maximum_convert_fusion, f32[3,512]{1,0:T(4,128)S(1)} %fusion.165, f32[3]{0:T(128)} %get-tuple-element.75, f32[512]{0:T(512)S(1)} %bitcast.106, f32[512]{0:T(512)S(1)} %bitcast.104, f32[512]{0:T(512)S(1)} %bitcast.102, f32[512]{0:T(512)S(1)} %bitcast.100, ...), kind=kLoop, calls=%fused_computation.266 | loop fusion | flops 5111808 | bytes 3188808 | tf_op jit(solution)/shard_map/add | solution.py:168
  93.6 5.9 %all-to-all-start = ((f32[3,32,512]{2,0,1:T(4,128)}), f32[3,32,512]{2,0,1:T(4,128)S(1)}, u32[]{:S(2)}, u32[]{:S(2)}) async-start(f32[3,32,512]{2,0,1:T(4,128)} %add_add_fusion), calls=%async_computation.2 | async-start | bytes 524288 | tf_op jit(solution)/shard_map/all_to_all | solution.py:240
  99.6 0.7 convert_element_type.107
  100.4 1.6 %fusion.161 = bf16[96,512]{1,0:T(8,128)(2,1)} fusion(f32[3,32,512]{2,1,0:T(8,128)S(1)} %copy.39, f32[96,512]{1,0:T(8,128)} %reduce-scatter.3.cloned.1.call-done, f32[512]{0:T(512)S(1)} %convert_element_type.107, f32[512]{0:T(512)S(1)} %dynamic_slice.38), kind=kLoop, calls=%fused_computation.271 | loop fusion | flops 196608 | bytes 495616 | tf_op jit(solution)/shard_map/convert_element_type | solution.py:147
  102.0 6.3 %all-to-all-done = f32[3,32,512]{2,0,1:T(4,128)S(1)} async-done(((f32[3,32,512]{2,0,1:T(4,128)}), f32[3,32,512]{2,0,1:T(4,128)S(1)}, u32[]{:S(2)}, u32[]{:S(2)}) %all-to-all-start) | async-done | bytes 196640 | tf_op jit(solution)/shard_map/all_to_all | solution.py:240
  108.3 0.8 copy.46
  (218 shorter events, 1.4 us)
Async XLA Ops:
  7.2 65.2 %reduce-scatter.5.cloned.1.call-start = ((), (), s32[]{:S(2)}) async-start(), calls=%async_computation.4 | async-start | bytes 294912 | tf_op jit(solution)/shard_map/reduce_scatter | solution.py:158
  8.2 21.2 %collective-permute-start = (bf16[3,4,512]{2,0,1:T(4,128)(2,1)S(1)}, bf16[3,4,512]{2,0,1:T(4,128)(2,1)S(1)}, u32[]{:S(2)}, u32[]{:S(2)}) collective-permute-start(bf16[3,4,512]{2,0,1:T(4,128)(2,1)S(1)} %copy.48), channel_id=1, source_target_pairs={{0,2},{2,0},{4,6},{6,4},{8,10},{10,8},{12,14},{14,12},{1,3},{3,1},... | collective-permute-start | bytes 36872 | tf_op jit(solution)/shard_map/ppermute | solution.py:21
  11.3 21.8 %collective-permute-start.1 = (bf16[3,4,512]{2,0,1:T(4,128)(2,1)S(1)}, bf16[3,4,512]{2,0,1:T(4,128)(2,1)S(1)}, u32[]{:S(2)}, u32[]{:S(2)}) collective-permute-start(bf16[3,4,512]{2,0,1:T(4,128)(2,1)S(1)} %copy.49), channel_id=1, source_target_pairs={{0,4},{2,6},{4,0},{6,2},{8,12},{10,14},{12,8},{14,10},{1,5},{3,7},... | collective-permute-start | bytes 36872 | tf_op jit(solution)/shard_map/ppermute | solution.py:21
  12.9 20.3 %collective-permute-start.2 = (bf16[3,4,512]{2,0,1:T(4,128)(2,1)S(1)}, bf16[3,4,512]{2,0,1:T(4,128)(2,1)S(1)}, u32[]{:S(2)}, u32[]{:S(2)}) collective-permute-start(bf16[3,4,512]{2,0,1:T(4,128)(2,1)S(1)} %copy.50), channel_id=1, source_target_pairs={{0,6},{2,4},{4,2},{6,0},{8,14},{10,12},{12,10},{14,8},{1,7},{3,5},... | collective-permute-start | bytes 36872 | tf_op jit(solution)/shard_map/ppermute | solution.py:21
  13.0 20.2 %collective-permute-start.3 = (bf16[3,4,512]{2,0,1:T(4,128)(2,1)S(1)}, bf16[3,4,512]{2,0,1:T(4,128)(2,1)S(1)}, u32[]{:S(2)}, u32[]{:S(2)}) collective-permute-start(bf16[3,4,512]{2,0,1:T(4,128)(2,1)S(1)} %copy.51), channel_id=1, source_target_pairs={{0,8},{2,10},{4,12},{6,14},{8,0},{10,2},{12,4},{14,6},{1,9},{3,11}... | collective-permute-start | bytes 36872 | tf_op jit(solution)/shard_map/ppermute | solution.py:21
  16.1 17.2 %collective-permute-start.4 = (bf16[3,4,512]{2,0,1:T(4,128)(2,1)S(1)}, bf16[3,4,512]{2,0,1:T(4,128)(2,1)S(1)}, u32[]{:S(2)}, u32[]{:S(2)}) collective-permute-start(bf16[3,4,512]{2,0,1:T(4,128)(2,1)S(1)} %copy.52), channel_id=1, source_target_pairs={{0,10},{2,8},{4,14},{6,12},{8,2},{10,0},{12,6},{14,4},{1,11},{3,9}... | collective-permute-start | bytes 36872 | tf_op jit(solution)/shard_map/ppermute | solution.py:21
  18.4 30.0 %copy-start.2 = (f32[1,1,512]{2,1,0:T(1,128)}, f32[1,1,512]{2,1,0:T(1,128)S(1)}, u32[]{:S(2)}) copy-start(f32[1,1,512]{2,1,0:T(1,128)S(1)} %get-tuple-element.65) | copy-start | bytes 6148
  18.4 30.0 %copy-start.4 = (f32[1,1,512]{2,1,0:T(1,128)}, f32[1,1,512]{2,1,0:T(1,128)S(1)}, u32[]{:S(2)}) copy-start(f32[1,1,512]{2,1,0:T(1,128)S(1)} %get-tuple-element.66) | copy-start | bytes 6148
  18.4 30.0 %copy-start.6 = (f32[1,1,512]{2,1,0:T(1,128)}, f32[1,1,512]{2,1,0:T(1,128)S(1)}, u32[]{:S(2)}) copy-start(f32[1,1,512]{2,1,0:T(1,128)S(1)} %get-tuple-element.67) | copy-start | bytes 6148
  19.6 28.8 %copy-start.8 = (f32[1,1,512]{2,1,0:T(1,128)}, f32[1,1,512]{2,1,0:T(1,128)S(1)}, u32[]{:S(2)}) copy-start(f32[1,1,512]{2,1,0:T(1,128)S(1)} %get-tuple-element.38) | copy-start | bytes 6148
  19.6 28.8 %copy-start.10 = (f32[1,1,512]{2,1,0:T(1,128)}, f32[1,1,512]{2,1,0:T(1,128)S(1)}, u32[]{:S(2)}) copy-start(f32[1,1,512]{2,1,0:T(1,128)S(1)} %get-tuple-element.39) | copy-start | bytes 6148
  19.6 28.8 %copy-start.12 = (f32[1,1,512]{2,1,0:T(1,128)}, f32[1,1,512]{2,1,0:T(1,128)S(1)}, u32[]{:S(2)}) copy-start(f32[1,1,512]{2,1,0:T(1,128)S(1)} %get-tuple-element.40) | copy-start | bytes 6148
  19.6 28.8 %copy-start.14 = (f32[1,1,512]{2,1,0:T(1,128)}, f32[1,1,512]{2,1,0:T(1,128)S(1)}, u32[]{:S(2)}) copy-start(f32[1,1,512]{2,1,0:T(1,128)S(1)} %get-tuple-element.41) | copy-start | bytes 6148
  19.6 28.8 %copy-start.16 = (f32[1,1,512]{2,1,0:T(1,128)}, f32[1,1,512]{2,1,0:T(1,128)S(1)}, u32[]{:S(2)}) copy-start(f32[1,1,512]{2,1,0:T(1,128)S(1)} %get-tuple-element.42) | copy-start | bytes 6148
  19.6 28.8 %copy-start.18 = (f32[1,1,512]{2,1,0:T(1,128)}, f32[1,1,512]{2,1,0:T(1,128)S(1)}, u32[]{:S(2)}) copy-start(f32[1,1,512]{2,1,0:T(1,128)S(1)} %get-tuple-element.43) | copy-start | bytes 6148
  19.6 28.8 %copy-start.20 = (f32[1,1,512]{2,1,0:T(1,128)}, f32[1,1,512]{2,1,0:T(1,128)S(1)}, u32[]{:S(2)}) copy-start(f32[1,1,512]{2,1,0:T(1,128)S(1)} %get-tuple-element.44) | copy-start | bytes 6148
  19.6 28.8 %copy-start.22 = (f32[1,1,512]{2,1,0:T(1,128)}, f32[1,1,512]{2,1,0:T(1,128)S(1)}, u32[]{:S(2)}) copy-start(f32[1,1,512]{2,1,0:T(1,128)S(1)} %get-tuple-element.45) | copy-start | bytes 6148
  19.6 28.8 %copy-start.24 = (f32[1,1,512]{2,1,0:T(1,128)}, f32[1,1,512]{2,1,0:T(1,128)S(1)}, u32[]{:S(2)}) copy-start(f32[1,1,512]{2,1,0:T(1,128)S(1)} %get-tuple-element.46) | copy-start | bytes 6148
  19.7 28.8 %copy-start.26 = (f32[1,1,512]{2,1,0:T(1,128)}, f32[1,1,512]{2,1,0:T(1,128)S(1)}, u32[]{:S(2)}) copy-start(f32[1,1,512]{2,1,0:T(1,128)S(1)} %get-tuple-element.47) | copy-start | bytes 6148
  19.7 28.8 %copy-start.28 = (f32[1,1,512]{2,1,0:T(1,128)}, f32[1,1,512]{2,1,0:T(1,128)S(1)}, u32[]{:S(2)}) copy-start(f32[1,1,512]{2,1,0:T(1,128)S(1)} %get-tuple-element.48) | copy-start | bytes 6148
  19.7 28.8 %copy-start.30 = (f32[1,1,512]{2,1,0:T(1,128)}, f32[1,1,512]{2,1,0:T(1,128)S(1)}, u32[]{:S(2)}) copy-start(f32[1,1,512]{2,1,0:T(1,128)S(1)} %get-tuple-element.49) | copy-start | bytes 6148
  19.7 28.8 %copy-start.32 = (f32[1,1,512]{2,1,0:T(1,128)}, f32[1,1,512]{2,1,0:T(1,128)S(1)}, u32[]{:S(2)}) copy-start(f32[1,1,512]{2,1,0:T(1,128)S(1)} %get-tuple-element.50) | copy-start | bytes 6148
  19.7 28.8 %copy-start.34 = (f32[1,1,512]{2,1,0:T(1,128)}, f32[1,1,512]{2,1,0:T(1,128)S(1)}, u32[]{:S(2)}) copy-start(f32[1,1,512]{2,1,0:T(1,128)S(1)} %get-tuple-element.51) | copy-start | bytes 6148
  19.7 28.8 %copy-start.36 = (f32[1,1,512]{2,1,0:T(1,128)}, f32[1,1,512]{2,1,0:T(1,128)S(1)}, u32[]{:S(2)}) copy-start(f32[1,1,512]{2,1,0:T(1,128)S(1)} %get-tuple-element.52) | copy-start | bytes 6148
  19.7 28.8 %copy-start.38 = (f32[1,1,512]{2,1,0:T(1,128)}, f32[1,1,512]{2,1,0:T(1,128)S(1)}, u32[]{:S(2)}) copy-start(f32[1,1,512]{2,1,0:T(1,128)S(1)} %get-tuple-element.53) | copy-start | bytes 6148
  19.7 28.8 %copy-start.40 = (f32[1,1,512]{2,1,0:T(1,128)}, f32[1,1,512]{2,1,0:T(1,128)S(1)}, u32[]{:S(2)}) copy-start(f32[1,1,512]{2,1,0:T(1,128)S(1)} %get-tuple-element.54) | copy-start | bytes 6148
  19.7 28.8 %copy-start.42 = (f32[1,1,512]{2,1,0:T(1,128)}, f32[1,1,512]{2,1,0:T(1,128)S(1)}, u32[]{:S(2)}) copy-start(f32[1,1,512]{2,1,0:T(1,128)S(1)} %get-tuple-element.55) | copy-start | bytes 6148
  19.7 28.8 %copy-start.44 = (f32[1,1,512]{2,1,0:T(1,128)}, f32[1,1,512]{2,1,0:T(1,128)S(1)}, u32[]{:S(2)}) copy-start(f32[1,1,512]{2,1,0:T(1,128)S(1)} %get-tuple-element.56) | copy-start | bytes 6148
  21.4 27.2 %copy-start.48 = (f32[1,1,512]{2,1,0:T(1,128)}, f32[1,1,512]{2,1,0:T(1,128)S(1)}, u32[]{:S(2)}) copy-start(f32[1,1,512]{2,1,0:T(1,128)S(1)} %get-tuple-element.20) | copy-start | bytes 6148
  21.4 27.2 %copy-start.50 = (f32[1,1,512]{2,1,0:T(1,128)}, f32[1,1,512]{2,1,0:T(1,128)S(1)}, u32[]{:S(2)}) copy-start(f32[1,1,512]{2,1,0:T(1,128)S(1)} %get-tuple-element.21) | copy-start | bytes 6148
  21.4 27.2 %copy-start.52 = (f32[1,1,512]{2,1,0:T(1,128)}, f32[1,1,512]{2,1,0:T(1,128)S(1)}, u32[]{:S(2)}) copy-start(f32[1,1,512]{2,1,0:T(1,128)S(1)} %get-tuple-element.22) | copy-start | bytes 6148
  21.4 27.2 %copy-start.54 = (f32[1,1,512]{2,1,0:T(1,128)}, f32[1,1,512]{2,1,0:T(1,128)S(1)}, u32[]{:S(2)}) copy-start(f32[1,1,512]{2,1,0:T(1,128)S(1)} %get-tuple-element.23) | copy-start | bytes 6148
  21.4 27.2 %copy-start.56 = (f32[1,1,512]{2,1,0:T(1,128)}, f32[1,1,512]{2,1,0:T(1,128)S(1)}, u32[]{:S(2)}) copy-start(f32[1,1,512]{2,1,0:T(1,128)S(1)} %get-tuple-element.24) | copy-start | bytes 6148
  21.4 27.2 %copy-start.58 = (f32[1,1,512]{2,1,0:T(1,128)}, f32[1,1,512]{2,1,0:T(1,128)S(1)}, u32[]{:S(2)}) copy-start(f32[1,1,512]{2,1,0:T(1,128)S(1)} %get-tuple-element.25) | copy-start | bytes 6148
  21.5 27.2 %copy-start.60 = (f32[1,1,512]{2,1,0:T(1,128)}, f32[1,1,512]{2,1,0:T(1,128)S(1)}, u32[]{:S(2)}) copy-start(f32[1,1,512]{2,1,0:T(1,128)S(1)} %get-tuple-element.26) | copy-start | bytes 6148
  21.5 27.2 %copy-start.62 = (f32[1,1,512]{2,1,0:T(1,128)}, f32[1,1,512]{2,1,0:T(1,128)S(1)}, u32[]{:S(2)}) copy-start(f32[1,1,512]{2,1,0:T(1,128)S(1)} %get-tuple-element.27) | copy-start | bytes 6148
  21.5 27.2 %copy-start.64 = (f32[1,1,512]{2,1,0:T(1,128)}, f32[1,1,512]{2,1,0:T(1,128)S(1)}, u32[]{:S(2)}) copy-start(f32[1,1,512]{2,1,0:T(1,128)S(1)} %get-tuple-element.28) | copy-start | bytes 6148
  21.5 27.2 %copy-start.66 = (f32[1,1,512]{2,1,0:T(1,128)}, f32[1,1,512]{2,1,0:T(1,128)S(1)}, u32[]{:S(2)}) copy-start(f32[1,1,512]{2,1,0:T(1,128)S(1)} %get-tuple-element.29) | copy-start | bytes 6148
  21.5 27.2 %copy-start.68 = (f32[1,1,512]{2,1,0:T(1,128)}, f32[1,1,512]{2,1,0:T(1,128)S(1)}, u32[]{:S(2)}) copy-start(f32[1,1,512]{2,1,0:T(1,128)S(1)} %get-tuple-element.30) | copy-start | bytes 6148
  21.5 27.2 %copy-start.70 = (f32[1,1,512]{2,1,0:T(1,128)}, f32[1,1,512]{2,1,0:T(1,128)S(1)}, u32[]{:S(2)}) copy-start(f32[1,1,512]{2,1,0:T(1,128)S(1)} %get-tuple-element.31) | copy-start | bytes 6148
  29.4 5.6 %collective-permute-start.5 = (bf16[3,4,512]{2,0,1:T(4,128)(2,1)S(1)}, bf16[3,4,512]{2,0,1:T(4,128)(2,1)S(1)}, u32[]{:S(2)}, u32[]{:S(2)}) collective-permute-start(bf16[3,4,512]{2,0,1:T(4,128)(2,1)S(1)} %copy.53), channel_id=1, source_target_pairs={{0,12},{2,14},{4,8},{6,10},{8,4},{10,6},{12,0},{14,2},{1,13},{3,15... | collective-permute-start | bytes 36872 | tf_op jit(solution)/shard_map/ppermute | solution.py:21
  33.1 6.5 %collective-permute-start.6 = (bf16[3,4,512]{2,0,1:T(4,128)(2,1)S(1)}, bf16[3,4,512]{2,0,1:T(4,128)(2,1)S(1)}, u32[]{:S(2)}, u32[]{:S(2)}) collective-permute-start(bf16[3,4,512]{2,0,1:T(4,128)(2,1)S(1)} %copy.54), channel_id=1, source_target_pairs={{0,14},{2,12},{4,10},{6,8},{8,6},{10,4},{12,2},{14,0},{1,15},{3,13... | collective-permute-start | bytes 36872 | tf_op jit(solution)/shard_map/ppermute | solution.py:21
  39.6 6.9 %collective-permute-start.8 = (bf16[3,32,512]{2,0,1:T(4,128)(2,1)S(1)}, bf16[3,32,512]{2,0,1:T(4,128)(2,1)S(1)}, u32[]{:S(2)}, u32[]{:S(2)}) collective-permute-start(bf16[3,32,512]{2,0,1:T(4,128)(2,1)S(1)} %constant_dynamic-update-slice_fusion), channel_id=1, source_target_pairs={{2,0},{4,2},{6,4},{8,6},{10,8},{12,10},{14,12},{3,1},{5,3},{7,5},{... | collective-permute-start | bytes 294920 | tf_op jit(solution)/shard_map/ppermute | solution.py:38
  40.9 7.1 %collective-permute-start.7 = (bf16[3,32,512]{2,0,1:T(4,128)(2,1)S(1)}, bf16[3,32,512]{2,0,1:T(4,128)(2,1)S(1)}, u32[]{:S(2)}, u32[]{:S(2)}) collective-permute-start(bf16[3,32,512]{2,0,1:T(4,128)(2,1)S(1)} %constant_dynamic-update-slice_fusion), channel_id=1, source_target_pairs={{0,2},{2,4},{4,6},{6,8},{8,10},{10,12},{12,14},{1,3},{3,5},{5,7},{... | collective-permute-start | bytes 294920 | tf_op jit(solution)/shard_map/ppermute | solution.py:36
  64.5 36.0 %reduce-scatter.3.cloned.1.call-start = ((), (), s32[]{:S(2)}) async-start(), calls=%async_computation.3 | async-start | bytes 589824 | tf_op jit(solution)/shard_map/reduce_scatter | solution.py:138
  77.1 10.2 %collective-permute-start.10 = (bf16[3,32,512]{2,0,1:T(4,128)(2,1)S(1)}, bf16[3,32,512]{2,0,1:T(4,128)(2,1)S(1)}, u32[]{:S(2)}, u32[]{:S(2)}) collective-permute-start(bf16[3,32,512]{2,0,1:T(4,128)(2,1)S(1)} %copy.43), channel_id=1, source_target_pairs={{2,0},{4,2},{6,4},{8,6},{10,8},{12,10},{14,12},{3,1},{5,3},{7,5},{... | collective-permute-start | bytes 294920 | tf_op jit(solution)/shard_map/ppermute | solution.py:38
  78.4 9.3 %collective-permute-start.9 = (bf16[3,32,512]{2,0,1:T(4,128)(2,1)S(1)}, bf16[3,32,512]{2,0,1:T(4,128)(2,1)S(1)}, u32[]{:S(2)}, u32[]{:S(2)}) collective-permute-start(bf16[3,32,512]{2,0,1:T(4,128)(2,1)S(1)} %copy.43), channel_id=1, source_target_pairs={{0,2},{2,4},{4,6},{6,8},{8,10},{10,12},{12,14},{1,3},{3,5},{5,7},{... | collective-permute-start | bytes 294920 | tf_op jit(solution)/shard_map/ppermute | solution.py:36
  93.6 14.7 %all-to-all-start = ((f32[3,32,512]{2,0,1:T(4,128)}), f32[3,32,512]{2,0,1:T(4,128)S(1)}, u32[]{:S(2)}, u32[]{:S(2)}) async-start(f32[3,32,512]{2,0,1:T(4,128)} %add_add_fusion), calls=%async_computation.2 | async-start | bytes 524288 | tf_op jit(solution)/shard_map/all_to_all | solution.py:240
  (53 other events, 261.3 us)
Sparse Core Ops, SparseCore 0:
  64.6 7.7 reduce-scatter.4
  87.4 8.8 reduce-scatter.2
